TPU v7x, 128 devices: a whole 4x4x4 slice. The times are simulated.
128 devices in a mesh: chan: 16 (over z, x_lo, core), seg: 8 (over y, x_hi).
Axes of the slice: x: 4 (x_hi: 2, x_lo: 2; x = x_hi * 2 + x_lo), y: 4, z: 4, core: 2. Of those that a mesh axis runs over, the one named last changes fastest.
Arguments:
- record: bfloat16 [144000, 6144], P('seg', 'chan'), may hold values from -24 to 24
- offsets: int32 [24], P('seg'), may hold values from 0 to 64
- bins: int32 [128], replicated, may hold values from 1 to 5999
- band_limit: int32 [6144], P('chan'), may hold values from 50 to 200
Outputs:
- stacked: bfloat16 [200, 2, 128, 6144], P(None, None, 'seg', 'chan')
All inputs are finite; a program needn't handle non-finite values.
Results may differ from a plain program's by a relative error of at most 0.0069.
Values may be sent and summed in bfloat16 or wider, within the bound.
A program may use at most 192 MiB of HBM per device.

v0:
```python
import math

import jax
import jax.numpy as jnp
from jax import lax
from jax.sharding import PartitionSpec as P

SEG_LEN = 12000
HOP = 6000
EXTRA = 6064
LAGS = 200


def from_behind(shard, axis, by):
    count = lax.axis_size(axis)
    pairs = [(i, i + by) for i in range(count) if 0 <= i + by < count]
    return lax.ppermute(shard, axis, pairs)


def table_of(bins):
    times = jnp.arange(SEG_LEN, dtype=jnp.int32)[:, None]
    phase = times * bins[None, :] % SEG_LEN
    angle = phase.astype(jnp.float32) * (2.0 * math.pi / SEG_LEN)
    return jnp.concatenate([jnp.cos(angle), -jnp.sin(angle)], axis=1).astype(jnp.bfloat16)


def transform(table, cleaned_rows):
    return lax.dot_general(
        table, cleaned_rows, (((0,), (0,)), ((), ())), preferred_element_type=jnp.float32
    )


def whiten(spectrum):
    power = jnp.mean(spectrum * spectrum, axis=0, keepdims=True)
    white = (spectrum * lax.rsqrt(power + 1e-06)).astype(jnp.bfloat16)
    return white.reshape(2, spectrum.shape[0] // 2, spectrum.shape[1])


def by_bin(parts_first):
    count, pairs, group, width = parts_first.shape
    return jnp.transpose(parts_first, (2, 1, 0, 3)).reshape(group, pairs * count, width)


def diagonals(product, lags):
    group, rows, width = product.shape
    flat = product.reshape(group, rows * width)
    flat = jnp.concatenate([flat, jnp.zeros((group, rows), product.dtype)], axis=1)
    return flat.reshape(group, rows, width + 1)[:, :, :lags]


def shards(record, offsets, bins, band_limit):
    time_dev, ch_dev = record.shape
    seg_dev = offsets.shape[0]
    total_channels = ch_dev * lax.axis_size("chan")
    segs_total = seg_dev * lax.axis_size("seg")
    table = table_of(bins)
    spectra_list = []
    rim_rows = from_behind(record[:EXTRA], "seg", -1)
    extended_rows = jnp.concatenate([record, rim_rows], axis=0)
    row_sums = jnp.sum(extended_rows, axis=1, dtype=jnp.float32)
    common = lax.psum(row_sums, "chan") / total_channels
    cleaned = (extended_rows.astype(jnp.float32) - common[:, None]).astype(jnp.bfloat16)
    for segment in range(seg_dev):
        start = segment * HOP + offsets[segment]
        rows = lax.dynamic_slice_in_dim(cleaned, start, SEG_LEN, 0)
        spectra_list.append(whiten(transform(table, rows)))
    spectra = jnp.stack(spectra_list)
    regrouped = lax.all_to_all(spectra, "seg", split_axis=2, concat_axis=0, tiled=True)
    neighbour = from_behind(regrouped[..., :LAGS], "chan", -1)
    extended = jnp.concatenate([regrouped, neighbour], axis=3)
    own_stack = by_bin(regrouped)
    turned = by_bin(jnp.stack([regrouped[:, 1], -regrouped[:, 0]], axis=1))
    ext_stack = by_bin(extended)
    real_full = jnp.einsum("fkc,fkd->fcd", own_stack, ext_stack, preferred_element_type=jnp.float32)
    imag_full = jnp.einsum("fkc,fkd->fcd", turned, ext_stack, preferred_element_type=jnp.float32)
    real_band = diagonals(real_full, LAGS)
    imag_band = diagonals(imag_full, LAGS)
    lag_index = jnp.arange(LAGS, dtype=jnp.int32)
    keep = (band_limit[:, None] >= lag_index[None, :]).astype(jnp.float32) / segs_total
    joined = jnp.stack([real_band, imag_band]) * keep[None, None, :, :]
    return jnp.transpose(joined, (3, 0, 1, 2)).astype(jnp.bfloat16)


def solution(mesh):
    return jax.shard_map(
        shards,
        mesh=mesh,
        in_specs=(P("seg", "chan"), P("seg"), P(), P("chan")),
        out_specs=P(None, None, "seg", "chan"),
        check_vma=False,
    )
```

profile of v0, /device:TPU:1, one launch (start us, length us, event | category | flops | bytes accessed | tf_op | source)
XLA Modules:
  0.0 535.0 jit_solution(3121954908515068144)
XLA Ops:
  6.5 0.0 all-reduce.4.cloned.1.call-start
  6.5 2.9 slice.27
  9.5 1.6 collective-permute-start
  11.0 0.0 copy-done.6
  11.1 26.7 %cosine_convert_fusion = (bf16[12000,128]{1,0:T(8,128)(2,1)S(1)}, bf16[12000,128]{1,0:T(8,128)(2,1)}) fusion(s32[128]{0:T(128)S(1)} %copy-done.6), kind=kLoop, calls=%fused_computation.20 | loop fusion | flops 18432000 | bytes 6144512 | tf_op jit(solution)/shard_map/convert
  37.8 77.4 %collective-permute-done = bf16[6064,384]{1,0:T(8,128)(2,1)S(1)} collective-permute-done((bf16[6064,384]{1,0:T(8,128)(2,1)S(1)}, bf16[6064,384]{1,0:T(8,128)(2,1)S(1)}, u32[]{:S(2)}, u32[]{:S(2)}) %collective-permute-start) | collective-permute-done | bytes 4657184 | tf_op jit(solution)/shard_map/ppermute | solution.py:17
  115.1 2.2 copy-done.1
  117.3 66.6 %convert_reduce_fusion = f32[24064]{0:T(1024)} fusion(bf16[6064,384]{1,0:T(8,128)(2,1)S(1)} %collective-permute-done, bf16[18000,384]{1,0:T(8,128)(2,1)S(1)} %copy-done), kind=kLoop, calls=%fused_computation.1 | loop fusion | flops 46178816 | bytes 18577408 | tf_op jit(solution)/shard_map/reduce_sum | solution.py:60
  183.9 0.0 all-reduce.4.cloned.1.call-update
  184.0 0.7 fusion.22
  188.9 110.6 %all-reduce.4.cloned.1.call-done = f32[24064]{0:T(1024)} async-done(((f32[24064]{0:T(1024)}), f32[24064]{0:T(1024)}) %all-reduce.4.cloned.1.call-update) | async-done | bytes 96272 | tf_op jit(solution)/shard_map/psum | solution.py:61
  299.4 0.9 broadcast_multiply_fusion
  300.3 0.0 copy-start.3
  300.4 20.9 %fusion = bf16[24064,384]{1,0:T(8,128)(2,1)} fusion(f32[24064]{0:T(1024)S(1)} %broadcast_multiply_fusion, bf16[6064,384]{1,0:T(8,128)(2,1)} %copy-done.1, bf16[18000,384]{1,0:T(8,128)(2,1)} %param.4), kind=kLoop, calls=%fused_computation.2 | loop fusion | flops 55443456 | bytes 37058560 | tf_op jit(solution)/shard_map/convert_element_type | solution.py:62
  321.3 7.3 %multiply_reduce_fusion.2 = (f32[384]{0:T(512)S(1)}, f32[256,384]{1,0:T(8,128)S(1)}) fusion(bf16[24064,384]{1,0:T(8,128)(2,1)} %fusion, s32[]{:T(128)S(6)} %select_n.17, bf16[12000,128]{1,0:T(8,128)(2,1)S(1)} %copy-done.3, bf16[12000,128]{1,0:T(8,128)(2,1)S(1)} %get-tuple-element.10), kind=kOutput, calls=%fused_computation.34 | convolution fusion | flops 2371780096 | bytes 15754756 | tf_op jit(solution)/shard_map/dot_general | solution.py:28
  328.6 0.2 copy.19
  328.8 1.3 copy-done.2
  330.2 3.5 multiply_reduce_fusion.1
  333.8 0.2 copy.20
  334.0 0.0 copy-start.5
  334.0 3.5 multiply_reduce_fusion
  337.5 0.2 copy.21
  337.8 1.9 pad_maximum_fusion.5
  339.6 6.5 %all-to-all-start = ((bf16[3,2,128,384]{3,1,0,2:T(2,128)(2,1)}), bf16[3,2,128,384]{3,1,0,2:T(2,128)(2,1)S(1)}, u32[]{:S(2)}, u32[]{:S(2)}) async-start(bf16[3,2,128,384]{3,1,0,2:T(2,128)(2,1)} %pad_maximum_fusion.5), calls=%async_computation | async-start | bytes 1179648 | tf_op jit(solution)/shard_map/all_to_all | solution.py:68
  346.2 0.0 copy-done.5
  346.2 0.1 fusion.14
  346.3 10.5 %all-to-all-done = bf16[3,2,128,384]{3,1,0,2:T(2,128)(2,1)S(1)} async-done(((bf16[3,2,128,384]{3,1,0,2:T(2,128)(2,1)}), bf16[3,2,128,384]{3,1,0,2:T(2,128)(2,1)S(1)}, u32[]{:S(2)}, u32[]{:S(2)}) %all-to-all-start) | async-done | bytes 589856 | tf_op jit(solution)/shard_map/all_to_all | solution.py:68
  356.8 0.1 copy.22
  356.9 0.1 copy.23
  357.0 4.5 collective-permute-start.1
  361.5 0.2 copy.24
  361.7 0.1 fusion.21
  361.8 0.1 maximum_bitcast_fusion.1
  361.8 0.2 copy.27
  362.0 4.1 collective-permute-done.1
  366.1 0.1 maximum_bitcast_fusion
  366.2 0.3 copy.25
  366.5 6.8 %fusion.23 = f32[16,384,584]{2,1,0:T(8,128)} fusion(bf16[16,48,384]{2,1,0:T(8,128)(2,1)S(1)} %bitcast.37, bf16[16,48,584]{2,1,0:T(8,128)(2,1)S(1)} %bitcast.35), kind=kOutput, calls=%fused_computation.49 | convolution fusion | flops 344457216 | bytes 15839232 | tf_op jit(solution)/shard_map/fkc,fkd->fcd/dot_general | solution.py:74
  373.3 22.4 %reshape.76 = f32[16,224256]{1,0:T(8,128)} reshape(f32[16,384,584]{2,1,0:T(8,128)} %fusion.23) | data formatting | bytes 28704768 | tf_op jit(solution)/shard_map/reshape | solution.py:46
  395.7 11.2 %concatenate.19 = f32[16,224640]{1,0:T(8,128)} pad(f32[16,224256]{1,0:T(8,128)} %reshape.76, f32[]{:T(128)} %constant.35.clone.1), padding=0_0x0_384 | pad | bytes 28729348 | tf_op jit(solution)/shard_map/concatenate | solution.py:47
  406.9 28.0 %reshape.77 = f32[16,384,585]{2,1,0:T(8,128)} reshape(f32[16,224640]{1,0:T(8,128)} %concatenate.19) | data formatting | bytes 28753920 | tf_op jit(solution)/shard_map/reshape | solution.py:48
  434.9 6.7 %fusion.24 = f32[16,384,584]{2,1,0:T(8,128)} fusion(bf16[16,48,384]{2,1,0:T(8,128)(2,1)S(1)} %bitcast.38, bf16[16,48,584]{2,1,0:T(8,128)(2,1)S(1)} %bitcast.36), kind=kOutput, calls=%fused_computation.50 | convolution fusion | flops 344457216 | bytes 15839232 | tf_op jit(solution)/shard_map/fkc,fkd->fcd/dot_general | solution.py:75
  441.5 22.8 %reshape.79 = f32[16,224256]{1,0:T(8,128)} reshape(f32[16,384,584]{2,1,0:T(8,128)} %fusion.24) | data formatting | bytes 28704768 | tf_op jit(solution)/shard_map/reshape | solution.py:46
  464.3 11.2 %concatenate.20 = f32[16,224640]{1,0:T(8,128)} pad(f32[16,224256]{1,0:T(8,128)} %reshape.79, f32[]{:T(128)} %constant.35.clone.1), padding=0_0x0_384 | pad | bytes 28729348 | tf_op jit(solution)/shard_map/concatenate | solution.py:47
  475.5 27.9 %reshape.80 = f32[16,384,585]{2,1,0:T(8,128)} reshape(f32[16,224640]{1,0:T(8,128)} %concatenate.20) | data formatting | bytes 28753920 | tf_op jit(solution)/shard_map/reshape | solution.py:48
  503.4 8.7 %slice_bitcast_fusion = (f32[1,16,384,200]{3,2,1,0:T(8,128)S(1)}, f32[1,16,384,200]{3,2,1,0:T(8,128)}) fusion(f32[16,384,585]{2,1,0:T(8,128)} %reshape.80, f32[16,384,585]{2,1,0:T(8,128)} %reshape.77), kind=kLoop, calls=%fused_computation.14 | loop fusion | bytes 19660800 | tf_op jit(solution)/shard_map/stack | solution.py:80
  512.1 7.2 %fusion.8 = bf16[200,2,16,384]{0,3,2,1:T(8,128)(2,1)} fusion(f32[1,16,384,200]{3,2,1,0:T(8,128)S(1)} %get-tuple-element.18, f32[1,16,384,200]{3,2,1,0:T(8,128)} %get-tuple-element.19, f32[384,200]{1,0:T(8,128)S(1)} %fusion.14), kind=kLoop, calls=%fused_computation.13 | loop fusion | flops 7372800 | bytes 15052800 | tf_op jit(solution)/shard_map/convert_element_type | solution.py:81
  519.3 8.7 %copy.29 = bf16[200,2,16,384]{3,2,1,0:T(8,128)(2,1)} copy(bf16[200,2,16,384]{0,3,2,1:T(8,128)(2,1)} %fusion.8) | data formatting | bytes 9830400 | tf_op jit(solution)/shard_map/convert_element_type | solution.py:81
  (15 shorter events, 0.2 us)
Async XLA Ops:
  6.5 4.5 copy-start.6
  6.5 292.9 %all-reduce.4.cloned.1.call-start = ((), (), s32[]{:S(2)}) async-start(), calls=%async_computation.1 | async-start | bytes 196608 | tf_op jit(solution)/shard_map/psum | solution.py:61
  6.5 110.8 %copy-start = (bf16[18000,384]{1,0:T(8,128)(2,1)S(1)}, bf16[18000,384]{1,0:T(8,128)(2,1)}, u32[]{:S(2)}) copy-start(bf16[18000,384]{1,0:T(8,128)(2,1)} %param.4) | copy-start | bytes 41472004
  9.5 105.7 %collective-permute-start = (bf16[6064,384]{1,0:T(8,128)(2,1)S(1)}, bf16[6064,384]{1,0:T(8,128)(2,1)S(1)}, u32[]{:S(2)}, u32[]{:S(2)}) collective-permute-start(bf16[6064,384]{1,0:T(8,128)(2,1)S(1)} %slice.27), channel_id=1, source_target_pairs={{1,0},{2,1},{3,2},{4,3},{5,4},{6,5},{7,6},{9,8},{10,9},{11,10},{12... | collective-permute-start | bytes 13971464 | tf_op jit(solution)/shard_map/ppermute | solution.py:17
  37.8 146.2 %copy-start.4 = (s32[3]{0:T(128)S(1)}, s32[3]{0:T(128)}, u32[]{:S(2)}) copy-start(s32[3]{0:T(128)} %param.5) | copy-start | bytes 40
  115.1 2.2 copy-start.1
  300.3 20.9 %copy-start.3 = (bf16[12000,128]{1,0:T(8,128)(2,1)S(1)}, bf16[12000,128]{1,0:T(8,128)(2,1)}, u32[]{:S(2)}) copy-start(bf16[12000,128]{1,0:T(8,128)(2,1)} %get-tuple-element.11) | copy-start | bytes 9216004
  321.3 8.9 %copy-start.2 = (bf16[24064,384]{1,0:T(8,128)(2,1)S(1)}, bf16[24064,384]{1,0:T(8,128)(2,1)}, u32[]{:S(2)}) copy-start(bf16[24064,384]{1,0:T(8,128)(2,1)} %fusion) | copy-start | bytes 55443460
  334.0 12.2 %copy-start.5 = (s32[384]{0:T(512)S(1)}, s32[384]{0:T(512)}, u32[]{:S(2)}) copy-start(s32[384]{0:T(512)} %param.7) | copy-start | bytes 4612
  339.6 17.2 %all-to-all-start = ((bf16[3,2,128,384]{3,1,0,2:T(2,128)(2,1)}), bf16[3,2,128,384]{3,1,0,2:T(2,128)(2,1)S(1)}, u32[]{:S(2)}, u32[]{:S(2)}) async-start(bf16[3,2,128,384]{3,1,0,2:T(2,128)(2,1)} %pad_maximum_fusion.5), calls=%async_computation | async-start | bytes 1179648 | tf_op jit(solution)/shard_map/all_to_all | solution.py:68
  357.0 9.1 %collective-permute-start.1 = (bf16[24,2,16,200]{3,2,1,0:T(8,128)(2,1)S(1)}, bf16[24,2,16,200]{3,2,1,0:T(8,128)(2,1)S(1)}, u32[]{:S(2)}, u32[]{:S(2)}) collective-permute-start(bf16[24,2,16,200]{3,2,1,0:T(8,128)(2,1)S(1)} %slice.36), channel_id=1, source_target_pairs={{8,0},{16,8},{24,16},{32,24},{40,32},{48,40},{56,48},{64,56},{72,6... | collective-permute-start | bytes 921608 | tf_op jit(solution)/shard_map/ppermute | solution.py:17
Sparse Core Ops, SparseCore 0:
  184.1 115.3 all-reduce.3
where the time goes:
time: 544 us; the launch traced here: 535 us
  waiting for transfers between devices  203 us (37%)
  local copies, waits for them, and re-layouts  149 us (27%)
  other arithmetic  125 us (23%)
  matrix products  27.7 us (5%)
  between operations  18.1 us (3%)
  starting transfers between devices  12.6 us (2%)
    psum x1, waiting for transfers between devices, shards(): common = lax.psum(row_sums, 'chan') / total_channels  111 us
    ppermute x2, waiting for transfers between devices, from_behind(): return lax.ppermute(shard, axis, pairs)  81.4 us
    reduce_sum x1, other arithmetic, shards(): row_sums = jnp.sum(extended_rows, axis=1, dtype=jnp.float32)  66.6 us
    reshape x2, local copies, waits for them, and re-layouts, diagonals(): return flat.reshape(group, rows, width + 1)[:, :, :lags]  55.9 us
    reshape x2, local copies, waits for them, and re-layouts, diagonals(): flat = product.reshape(group, rows * width)  45.1 us
    another operation x1, other arithmetic  26.7 us
    concatenate x2, local copies, waits for them, and re-layouts, diagonals(): jnp.concatenate([flat, jnp.zeros((group, rows), product.dtype)], axis=1)  22.4 us
    convert_element_type x1, other arithmetic, shards(): (extended_rows.astype(jnp.float32) - common[:, None]).astype(jnp.bfloat16)  20.9 us
  transfers between devices with their start and end apart: 4, of which 4 were waited for; matrix products, arithmetic and copies ran while one was open for 5% of the time, Pallas kernels for 0%

commit v1 on v0

v1 whole, which is shorter than its diff:
```python
import math

import jax
import jax.numpy as jnp
from jax import lax
from jax.experimental import pallas as pl
from jax.experimental.pallas import tpu as pltpu
from jax.sharding import PartitionSpec as P

SEG_LEN = 12000
HOP = 6000
LAGS = 200
RIM = 128
CHUNK = 1024
CHUNKS = -(-HOP // CHUNK)
BLOCKS = CHUNK // 128
LAST = HOP - CHUNK
VMEM_LIMIT = 60 * 1024 * 1024
F32 = jnp.float32
BF16 = jnp.bfloat16


def dot(a, b, dims):
    return lax.dot_general(a, b, (dims, ((), ())), preferred_element_type=F32)


def dft_kernel(offs_ref, bins_ref, rec_ref, nxt_ref, out_ref, x_ref, fine, coarse, w_ref, acc, sems):
    def piece(i, block):
        lo = CHUNK * i
        size = min(CHUNK, HOP - lo)
        rows = pl.ds(HOP * block + lo, size)
        return pltpu.make_async_copy(rec_ref.at[rows], x_ref.at[rows], sems.at[i, block])

    for i in range(CHUNKS):
        for block in range(3):
            piece(i, block).start()

    bcol = jnp.transpose(jnp.broadcast_to(bins_ref[...].astype(F32), (128, 128))).astype(jnp.int32)
    lane = lax.broadcasted_iota(jnp.int32, (128, 128), 1)

    def phasor(times):
        phase = (bcol * times) % SEG_LEN
        angle = phase.astype(F32) * (2.0 * math.pi / SEG_LEN)
        return jnp.cos(angle), -jnp.sin(angle)

    base_c, base_s = phasor(lane)
    column = lane - BLOCKS
    owner = column // CHUNKS
    step = column - owner * CHUNKS
    start = jnp.minimum(step * CHUNK, LAST)
    shift = jnp.where(
        owner == 0,
        offs_ref[0],
        jnp.where(owner == 1, offs_ref[1], jnp.where(owner == 2, offs_ref[2], offs_ref[3])),
    )
    times = jnp.where(lane < BLOCKS, lane * 128, start - shift + SEG_LEN)
    times = jnp.where(lane < BLOCKS + 4 * CHUNKS, times, 0) % SEG_LEN
    mult_c, mult_s = phasor(times)

    def spread(values, index):
        return jnp.broadcast_to(values[:, index : index + 1], (128, 128))

    def rotate(ac, as_, bc, bs):
        return ac * bc - as_ * bs, as_ * bc + ac * bs

    for m in range(BLOCKS):
        c, s = rotate(spread(mult_c, m), spread(mult_s, m), base_c, base_s)
        fine[0, m] = c
        fine[1, m] = s
    for q in range(4 * CHUNKS):
        coarse[q, 0] = spread(mult_c, BLOCKS + q)
        coarse[q, 1] = spread(mult_s, BLOCKS + q)

    acc[...] = jnp.zeros_like(acc)

    def chunk(i, carry):
        first = jnp.minimum(i * CHUNK, LAST)
        skip = i * CHUNK - first
        for block in range(3):
            for j in range(CHUNKS):
                @pl.when(i == j)
                def _():
                    piece(j, block).wait()
        for o in range(4):
            ec = coarse[o * CHUNKS + i, 0]
            es = coarse[o * CHUNKS + i, 1]
            for m in range(BLOCKS):
                c, s = rotate(ec, es, fine[0, m], fine[1, m])
                if m < 2:
                    live = lane + 128 * m >= skip
                    c = jnp.where(live, c, 0.0)
                    s = jnp.where(live, s, 0.0)
                w_ref[pl.ds(256 * o, 128), pl.ds(128 * m, 128)] = c.astype(BF16)
                w_ref[pl.ds(256 * o + 128, 128), pl.ds(128 * m, 128)] = s.astype(BF16)
        for block in range(3):
            rows = x_ref[pl.ds(pl.multiple_of(HOP * block + first, 16), CHUNK), :]
            acc[block] += dot(w_ref[pl.ds(256 * block, 512), :], rows, ((1,), (0,)))
        return carry

    lax.fori_loop(0, CHUNKS, chunk, 0)

    def head(o):
        c, s = rotate(coarse[o * CHUNKS, 0], coarse[o * CHUNKS, 1], fine[0, 0], fine[1, 0])
        live = lane < offs_ref[o]
        zero = jnp.zeros_like(c)
        return jnp.concatenate([jnp.where(live, c, zero), jnp.where(live, s, zero)], axis=0)

    def first_rows(block):
        return x_ref[pl.ds(HOP * block, RIM), :]

    def swap(o, new, old):
        w = head(o).astype(BF16)
        both = jnp.concatenate([w, -w], axis=1)
        return dot(both, jnp.concatenate([new, old], axis=0), ((1,), (0,)))

    odd = jnp.concatenate([bcol, bcol], axis=0) % 2
    sign = (1 - 2 * odd).astype(F32)
    sign = jnp.concatenate([sign, sign, sign], axis=1)
    out_ref[0] = sign * acc[0, :256] + dot(head(0).astype(BF16), first_rows(1), ((1,), (0,)))
    out_ref[1] = acc[0, 256:] + sign * acc[1, :256] + swap(1, first_rows(2), first_rows(0))
    out_ref[2] = acc[1, 256:] + sign * acc[2, :256] + swap(2, nxt_ref[...], first_rows(1))
    out_ref[3] = acc[2, 256:] - dot(head(3).astype(BF16), first_rows(2), ((1,), (0,)))


def partial_spectra(offs, bins, record, nxt):
    width = record.shape[1]
    vmem = pl.BlockSpec(memory_space=pltpu.VMEM)
    return pl.pallas_call(
        dft_kernel,
        out_shape=jax.ShapeDtypeStruct((4, 256, width), F32),
        in_specs=[pl.BlockSpec(memory_space=pltpu.SMEM), vmem, pl.BlockSpec(memory_space=pl.ANY), vmem],
        out_specs=vmem,
        scratch_shapes=[
            pltpu.VMEM(record.shape, BF16),
            pltpu.VMEM((2, BLOCKS, 128, 128), F32),
            pltpu.VMEM((4 * CHUNKS, 2, 128, 128), F32),
            pltpu.VMEM((1024, CHUNK), BF16),
            pltpu.VMEM((3, 512, width), F32),
            pltpu.SemaphoreType.DMA((CHUNKS, 3)),
        ],
        compiler_params=pltpu.CompilerParams(vmem_limit_bytes=VMEM_LIMIT),
        name="dft",
    )(offs, bins, record, nxt)


def band_kernel(scale, ext_ref, limit_ref, out_ref, own, rev, wide):
    tile = pl.program_id(0)
    rows = own.shape[1]
    segs = rows // 32

    @pl.when(tile == 0)
    def _():
        size = rev.shape[0] * 128
        at = lax.broadcasted_iota(jnp.int32, (size, size), 0)
        to = lax.broadcasted_iota(jnp.int32, (size, size), 1)
        flip = (at + to == size - 1).astype(BF16)
        turned = dot(ext_ref[...], flip, ((1,), (0,)))
        for t in range(rev.shape[0]):
            rev[t] = turned[:, 128 * t : 128 * t + 128]
        for t in range(own.shape[0]):
            own[t] = ext_ref[:, 128 * t : 128 * t + 128].astype(F32)

    lag = lax.broadcasted_iota(jnp.int32, (208, 256), 0)
    spot = lax.broadcasted_iota(jnp.int32, (208, 256), 1)
    pick = (lag + spot == 255).astype(BF16)
    back = own.shape[0] - 1 - tile

    def one_bin(f, carry):
        real = own[tile, pl.ds(f, segs, stride=32), :]
        imag = own[tile, pl.ds(16 + f, segs, stride=32), :]
        lhs = jnp.concatenate(
            [jnp.concatenate([real, imag], axis=0), jnp.concatenate([imag, -real], axis=0)], axis=1
        ).astype(BF16)
        other = []
        for t in range(3):
            other.append(
                jnp.concatenate(
                    [rev[back + t, pl.ds(f, segs, stride=32), :], rev[back + t, pl.ds(16 + f, segs, stride=32), :]],
                    axis=0,
                )
            )
        rhs = jnp.concatenate(other, axis=1).astype(BF16)
        product = dot(lhs, rhs, ((0,), (0,)))
        lined = []
        for p in range(2):
            rolled = pltpu.roll(product[128 * p : 128 * p + 128], 0, 1, stride=1, stride_axis=0)
            lined.append((rolled[:, 128:] * scale).astype(BF16))
        by_lag = dot(pick, jnp.concatenate(lined, axis=0), ((1,), (1,)))
        wide[pl.ds(f, LAGS, stride=32), :] = by_lag[:LAGS, :128]
        wide[pl.ds(16 + f, LAGS, stride=32), :] = by_lag[:LAGS, 128:]
        return carry

    lax.fori_loop(0, 16, one_bin, 0)
    limit = jnp.broadcast_to(limit_ref[...], (32, 128))

    def store(j, carry):
        for n in range(8):
            k = j * 8 + n
            values = wide[pl.ds(pl.multiple_of(k * 32, 32), 32), :]
            values = jnp.where(limit >= k, values, 0.0).astype(BF16)
            out_ref[k, 0] = values[:16]
            out_ref[k, 1] = values[16:]
        return carry

    lax.fori_loop(0, LAGS // 8, store, 0)


def band(ext, limit, segs, width):
    rows, reach = ext.shape
    return pl.pallas_call(
        lambda *refs: band_kernel(1.0 / segs, *refs),
        grid=(width // 128,),
        out_shape=jax.ShapeDtypeStruct((LAGS, 2, 16, width), BF16),
        in_specs=[
            pl.BlockSpec((rows, reach), lambda i: (0, 0)),
            pl.BlockSpec((1, 128), lambda i: (0, i)),
        ],
        out_specs=pl.BlockSpec((LAGS, 2, 16, 128), lambda i: (0, 0, 0, i)),
        scratch_shapes=[
            pltpu.VMEM((width // 128, rows, 128), F32),
            pltpu.VMEM((reach // 128, rows, 128), F32),
            pltpu.VMEM((LAGS * 32, 128), F32),
        ],
        compiler_params=pltpu.CompilerParams(vmem_limit_bytes=VMEM_LIMIT),
        name="band",
    )(ext, limit)


def along(shard, axis, by):
    count = lax.axis_size(axis)
    pairs = [(i, i + by) for i in range(count) if 0 <= i + by < count]
    return lax.ppermute(shard, axis, pairs)


def shards(record, offsets, bins, band_limit):
    width = record.shape[1]
    segs = offsets.shape[0] * lax.axis_size("seg")
    channels = width * lax.axis_size("chan")
    nxt = along(record[:RIM], "seg", -1)
    before = along(offsets, "seg", 1)
    offs = jnp.concatenate([before[2:], offsets])
    parts = partial_spectra(offs, bins[None, :], record, nxt)
    rest = along(parts[0], "seg", -1)
    spectra = jnp.stack([parts[1], parts[2], parts[3] + rest])
    mean = lax.psum(jnp.sum(spectra, axis=2), "chan") / channels
    spectra = spectra - mean[:, :, None]
    power = jnp.mean(spectra * spectra, axis=1, keepdims=True)
    white = (spectra * lax.rsqrt(power + 1e-06)).astype(BF16).reshape(3, 2, 128, width)
    regrouped = lax.all_to_all(white, "seg", split_axis=2, concat_axis=0, tiled=True)
    neighbour = along(regrouped[..., :256], "chan", -1)
    ext = jnp.concatenate([regrouped, neighbour], axis=3)
    return band(ext.reshape(segs * 32, width + 256), band_limit[None, :], segs, width)


def solution(mesh):
    return jax.shard_map(
        shards,
        mesh=mesh,
        in_specs=(P("seg", "chan"), P("seg"), P(), P("chan")),
        out_specs=P(None, None, "seg", "chan"),
        check_vma=False,
    )
```

time: 544 us -> 142 us (0.26); the launches traced: 535 us -> 141 us
  waiting for transfers between devices: 203 us -> 15.7 us
  local copies, waits for them, and re-layouts: 149 us -> 6.18 us
  other arithmetic: 125 us -> 5.16 us
  Pallas kernels: 0 us -> 52.9 us
  blocking collectives: 0 us -> 48.2 us
  matrix products: 27.7 us -> 0 us
  between operations: 18.1 us -> 0.15 us
    psum x1 -> x0, waiting for transfers between devices: 111 us -> none  [shards(): common = lax.psum(row_sums, 'chan') / total_channels]
    reshape x4 -> x0, local copies, waits for them, and re-layouts: 101 us -> none  [the longest x2 55.9 us: diagonals(): return flat.reshape(group, rows, width + 1)[:, :, :lags]]
    reduce_sum x1 -> x2, other arithmetic: 66.6 us -> 0.38 us  [the longest x1 0.2 us: shards(): power = jnp.mean(spectra * spectra, axis=1, keepdims=True)]
    ppermute x2 -> x4, waiting for transfers between devices: 81.4 us -> 15.7 us  [along(): return lax.ppermute(shard, axis, pairs)]
    pallas_call x0 -> x2, Pallas kernels: none -> 52.9 us  [the longest x1 36.1 us: band(): pl.pallas_call(lambda *refs: band_kernel(1.0 / segs, *refs), grid=(width...]
    psum x0 -> x1, blocking collectives: none -> 29.9 us  [shards(): mean = lax.psum(jnp.sum(spectra, axis=2), 'chan') / channels]
    another operation x2 -> x0, other arithmetic: 28.6 us -> none
    dot_general x5 -> x0, matrix products: 27.7 us -> none  [the longest x3 14.3 us: transform(): lax.dot_general(table, cleaned_rows, (((0,), (0,)), ((), ())), preferred_...]
  transfers between devices with their start and end apart: 4 -> 4, of which waited for: 4 -> 3; matrix products, arithmetic and copies ran while one was open for 5% -> 4% of each run, Pallas kernels for 0% -> 0%
where the time goes in v1:
time: 142 us; the launch traced here: 141 us
  Pallas kernels  52.9 us (37%)
  blocking collectives  48.2 us (34%)
  waiting for transfers between devices  15.7 us (11%)
  starting transfers between devices  12.8 us (9%)
  local copies, waits for them, and re-layouts  6.18 us (4%)
  other arithmetic  5.16 us (4%)
    pallas_call x1, Pallas kernels, band(): pl.pallas_call(lambda *refs: band_kernel(1.0 / segs, *refs), grid=(width...  36.1 us
    psum x1, blocking collectives, shards(): mean = lax.psum(jnp.sum(spectra, axis=2), 'chan') / channels  29.9 us
    all_to_all x1, blocking collectives, shards(): lax.all_to_all(white, 'seg', split_axis=2, concat_axis=0, tiled=True)  18.4 us
    pallas_call x1, Pallas kernels, partial_spectra(): pl.pallas_call(dft_kernel, out_shape=jax.ShapeDtypeStruct((4, 256, width)...  16.8 us
    ppermute x4, waiting for transfers between devices, along(): return lax.ppermute(shard, axis, pairs)  15.7 us
    ppermute x4, starting transfers between devices, along(): return lax.ppermute(shard, axis, pairs)  12.8 us
  transfers between devices with their start and end apart: 4, of which 3 were waited for; matrix products, arithmetic and copies ran while one was open for 4% of the time, Pallas kernels for 0%

profile of v1, /device:TPU:1, one launch (start us, length us, event | category | flops | bytes accessed | tf_op | source)
XLA Modules:
  0.0 141.1 jit_solution(13376717532717875127)
XLA Ops:
  0.0 5.5 %collective-permute-start = (s32[3]{0:T(128)}, s32[3]{0:T(128)S(1)}, u32[]{:S(2)}, u32[]{:S(2)}) collective-permute-start(s32[3]{0:T(128)} %param.5), channel_id=1, source_target_pairs={{0,1},{1,2},{2,3},{3,4},{4,5},{5,6},{6,7},{8,9},{9,10},{10,11},{11... | collective-permute-start | bytes 44 | tf_op jit(solution)/shard_map/ppermute | solution.py:232
  5.5 0.9 slice.21
  6.4 1.3 collective-permute-start.1
  7.7 0.0 collective-permute-done
  7.7 0.6 slice.20
  8.3 1.9 %pad_add_fusion.offs_ref = s32[4]{0:T(128)} fusion(s32[3]{0:T(128)} %param.5, s32[1]{0:T(128)} %slice.20), kind=kLoop, calls=%fused_computation.12 | loop fusion | flops 4 | bytes 32 | tf_op jit(solution)/shard_map/concatenate | solution.py:241
  10.1 3.1 %collective-permute-done.1.nxt_ref = bf16[128,384]{1,0:T(8,128)(2,1)S(1)} collective-permute-done((bf16[128,384]{1,0:T(8,128)(2,1)S(1)}, bf16[128,384]{1,0:T(8,128)(2,1)S(1)}, u32[]{:S(2)}, u32[]{:S(2)}) %collective-permute-start.1) | collective-permute-done | bytes 98336 | tf_op jit(solution)/shard_map/ppermute | solution.py:232
  13.2 0.0 copy-start
  13.2 0.6 copy-done
  13.9 16.8 %dft.1 = f32[4,256,384]{2,1,0:T(8,128)} custom-call(s32[4]{0:T(128)} %pad_add_fusion.offs_ref, s32[1,128]{1,0:T(1,128)} %bitcast.24, bf16[18000,384]{1,0:T(8,128)(2,1)} %rec_ref.1, bf16[128,384]{1,0:T(8,128)(2,1)} %copy-done), custom_call_target="tpu_custom_call" | custom-call | tf_op jit(solution)/shard_map/dft/pallas_call | solution.py:128
  30.7 1.0 slice_bitcast_fusion
  31.7 1.3 collective-permute-start.2
  33.0 1.2 slice.26
  34.2 0.6 copy.8
  34.8 8.9 %collective-permute-done.2 = f32[256,384]{1,0:T(8,128)S(1)} collective-permute-done((f32[256,384]{1,0:T(8,128)S(1)}, f32[256,384]{1,0:T(8,128)S(1)}, u32[]{:S(2)}, u32[]{:S(2)}) %collective-permute-start.2) | collective-permute-done | bytes 393248 | tf_op jit(solution)/shard_map/ppermute | solution.py:232
  43.7 1.0 fusion.3
  44.7 0.2 fusion.2
  44.9 29.9 %psum.7 = f32[3,256]{1,0:T(4,128)S(1)} all-reduce(f32[3,256]{1,0:T(4,128)S(1)} %fusion.2), channel_id=1, replica_groups=mesh['chan'=16,'seg'=8] {'chan'}, use_global_device_ids=true, to_apply=%region_1.0 | all-reduce | flops 768 | bytes 6144 | tf_op jit(solution)/shard_map/psum | solution.py:245
  74.8 0.2 multiply_reduce_fusion
  75.0 0.2 copy.10
  75.2 0.3 copy.9
  75.5 0.8 fusion.1
  76.3 18.4 %all_to_all.18 = bf16[3,2,128,384]{3,1,0,2:T(2,128)(2,1)S(1)} all-to-all(bf16[3,2,128,384]{3,1,0,2:T(2,128)(2,1)S(1)} %fusion.1), channel_id=1, replica_groups=mesh['chan'=16,'seg'=8] {'seg'}, dimensions={2} | all-to-all | bytes 1179648 | tf_op jit(solution)/shard_map/all_to_all | solution.py:249
  94.7 0.1 copy.11
  94.8 0.0 copy-start.1
  94.8 0.1 copy.12
  94.9 4.8 %collective-permute-start.3 = (bf16[24,2,16,256]{3,2,1,0:T(8,128)(2,1)S(1)}, bf16[24,2,16,256]{3,2,1,0:T(8,128)(2,1)S(1)}, u32[]{:S(2)}, u32[]{:S(2)}) collective-permute-start(bf16[24,2,16,256]{3,2,1,0:T(8,128)(2,1)S(1)} %slice.29), channel_id=1, source_target_pairs={{8,0},{16,8},{24,16},{32,24},{40,32},{48,40},{56,48},{64,56},{72,6... | collective-permute-start | bytes 1179656 | tf_op jit(solution)/shard_map/ppermute | solution.py:232
  99.7 0.0 copy-done.1
  99.7 0.6 broadcast_in_dim.9.refs_1_
  100.3 3.7 %collective-permute-done.3 = bf16[24,2,16,256]{3,2,1,0:T(8,128)(2,1)S(1)} collective-permute-done((bf16[24,2,16,256]{3,2,1,0:T(8,128)(2,1)S(1)}, bf16[24,2,16,256]{3,2,1,0:T(8,128)(2,1)S(1)}, u32[]{:S(2)}, u32[]{:S(2)}) %collective-permute-start.3) | collective-permute-done | bytes 393248 | tf_op jit(solution)/shard_map/ppermute | solution.py:232
  104.0 1.1 pad_maximum_fusion.1.refs_0_
  105.0 36.1 %band.1 = bf16[200,2,16,384]{3,2,1,0:T(8,128)(2,1)} custom-call(bf16[768,640]{1,0:T(8,128)(2,1)} %pad_maximum_fusion.1.refs_0_, s32[1,384]{1,0:T(1,128)} %broadcast_in_dim.9.refs_1_), custom_call_target="tpu_custom_call" | custom-call | tf_op jit(solution)/shard_map/band/pallas_call | solution.py:210
  (4 shorter events, 0.1 us)
Async XLA Ops:
  0.0 7.7 %collective-permute-start = (s32[3]{0:T(128)}, s32[3]{0:T(128)S(1)}, u32[]{:S(2)}, u32[]{:S(2)}) collective-permute-start(s32[3]{0:T(128)} %param.5), channel_id=1, source_target_pairs={{0,1},{1,2},{2,3},{3,4},{4,5},{5,6},{6,7},{8,9},{9,10},{10,11},{11... | collective-permute-start | bytes 44 | tf_op jit(solution)/shard_map/ppermute | solution.py:232
  6.4 6.9 %collective-permute-start.1 = (bf16[128,384]{1,0:T(8,128)(2,1)S(1)}, bf16[128,384]{1,0:T(8,128)(2,1)S(1)}, u32[]{:S(2)}, u32[]{:S(2)}) collective-permute-start(bf16[128,384]{1,0:T(8,128)(2,1)S(1)} %slice.21), channel_id=1, source_target_pairs={{1,0},{2,1},{3,2},{4,3},{5,4},{6,5},{7,6},{9,8},{10,9},{11,10},{12... | collective-permute-start | bytes 294920 | tf_op jit(solution)/shard_map/ppermute | solution.py:232
  13.2 0.6 copy-start
  31.7 12.0 %collective-permute-start.2 = (f32[256,384]{1,0:T(8,128)S(1)}, f32[256,384]{1,0:T(8,128)S(1)}, u32[]{:S(2)}, u32[]{:S(2)}) collective-permute-start(f32[256,384]{1,0:T(8,128)S(1)} %slice_bitcast_fusion), channel_id=1, source_target_pairs={{1,0},{2,1},{3,2},{4,3},{5,4},{6,5},{7,6},{9,8},{10,9},{11,10},{12... | collective-permute-start | bytes 1179656 | tf_op jit(solution)/shard_map/ppermute | solution.py:232
  94.8 4.9 %copy-start.1 = (s32[384]{0:T(512)S(1)}, s32[384]{0:T(512)}, u32[]{:S(2)}) copy-start(s32[384]{0:T(512)} %param.7) | copy-start | bytes 4612
  94.9 9.1 %collective-permute-start.3 = (bf16[24,2,16,256]{3,2,1,0:T(8,128)(2,1)S(1)}, bf16[24,2,16,256]{3,2,1,0:T(8,128)(2,1)S(1)}, u32[]{:S(2)}, u32[]{:S(2)}) collective-permute-start(bf16[24,2,16,256]{3,2,1,0:T(8,128)(2,1)S(1)} %slice.29), channel_id=1, source_target_pairs={{8,0},{16,8},{24,16},{32,24},{40,32},{48,40},{56,48},{64,56},{72,6... | collective-permute-start | bytes 1179656 | tf_op jit(solution)/shard_map/ppermute | solution.py:232

commit v2 on v1

v2 whole, which is shorter than its diff:
```python
import functools
import math

import jax
import jax.numpy as jnp
from jax import lax
from jax.experimental import pallas as pl
from jax.experimental.pallas import tpu as pltpu
from jax.sharding import PartitionSpec as P

SEG_LEN = 12000
HOP = 6000
LAGS = 200
PITCH = 33
UNROLL = 4
RIM = 64
CHUNK = 1024
CHUNKS = -(-HOP // CHUNK)
BLOCKS = CHUNK // 128
LAST = HOP - CHUNK
VMEM_LIMIT = 60 * 1024 * 1024
F32 = jnp.float32
BF16 = jnp.bfloat16
MESH = pl.DeviceIdType.MESH


def dot(a, b, dims):
    return lax.dot_general(a, b, (dims, ((), ())), preferred_element_type=F32)


def spectra_kernel(
    chans, segs, offs_ref, bins_ref, rec_ref, out_ref,
    x_ref, fine, coarse, w_ref, acc, accs, spec, head, lump, first_sum, first_sums, own_sum, own_sums,
    rim, rest, white, got,
    local_sem, rim_send, rim_recv, lump_send, lump_recv, first_send, first_recv, sum_send, sum_recv,
    part_send, part_recv, near_send, near_recv,
):
    me_c = lax.axis_index("chan")
    me_s = lax.axis_index("seg")
    before = (me_s + segs - 1) % segs
    after = (me_s + 1) % segs
    left = (me_c + chans - 1) % chans
    width = x_ref.shape[1]

    rim[:, RIM:, :] = jnp.zeros((2, 128 - RIM, width), BF16)

    barrier = pltpu.get_barrier_semaphore()

    def greet(c, g):
        pl.semaphore_signal(barrier, inc=1, device_id={"chan": c, "seg": g}, device_id_type=MESH)

    def greet_chan(i, carry):
        c = (me_c + i) % chans
        greet(c, me_s)
        greet(c, before)
        greet(c, after)
        return carry

    def greet_seg(i, carry):
        greet(me_c, (me_s + i) % segs)
        return carry

    lax.fori_loop(1, chans, greet_chan, 0)
    lax.fori_loop(1, segs, greet_seg, 0)

    def piece(block, i, size):
        rows = pl.ds(pl.multiple_of(HOP * block + CHUNK * i, 16), size)
        return pltpu.make_async_copy(rec_ref.at[rows], x_ref.at[rows], local_sem.at[block, i])

    for block in range(3):
        for i in range(CHUNKS):
            piece(block, i, CHUNK if i < CHUNKS - 1 else HOP - CHUNK * (CHUNKS - 1)).start()

    bcol = jnp.transpose(jnp.broadcast_to(bins_ref[...].astype(F32), (128, 128))).astype(jnp.int32)
    lane = lax.broadcasted_iota(jnp.int32, (128, 128), 1)

    def phasor(times):
        phase = (bcol * times) % SEG_LEN
        angle = phase.astype(F32) * (2.0 * math.pi / SEG_LEN)
        return jnp.cos(angle), -jnp.sin(angle)

    base_c, base_s = phasor(lane)
    times = jnp.where(lane < BLOCKS, lane * 128, jnp.minimum((lane - BLOCKS) * CHUNK, LAST))
    for q in range(3):
        times = jnp.where(lane == BLOCKS + CHUNKS + q, SEG_LEN - offs_ref[q], times)
    mult_c, mult_s = phasor(times % SEG_LEN)

    def spread(values, index):
        return jnp.broadcast_to(values[:, index : index + 1], (128, 128))

    def rotate(ac, as_, bc, bs):
        return ac * bc - as_ * bs, as_ * bc + ac * bs

    for m in range(BLOCKS):
        c, s = rotate(spread(mult_c, m), spread(mult_s, m), base_c, base_s)
        fine[0, m] = c
        fine[1, m] = s
    for q in range(CHUNKS + 3):
        coarse[q, 0] = spread(mult_c, BLOCKS + q)
        coarse[q, 1] = spread(mult_s, BLOCKS + q)
    odd = bcol % 2
    sign = (1 - 2 * odd).astype(F32)

    pl.semaphore_wait(barrier, 3 * (chans - 1) + segs - 1)

    def send_rim(k):
        return pltpu.make_async_remote_copy(
            src_ref=rec_ref.at[pl.ds(HOP * k, RIM)],
            dst_ref=rim.at[k, pl.ds(0, RIM)],
            send_sem=rim_send.at[k],
            recv_sem=rim_recv.at[k],
            device_id={"chan": me_c, "seg": before},
            device_id_type=MESH,
        )

    for k in range(2):
        send_rim(k).start()

    acc[...] = jnp.zeros_like(acc)
    accs[...] = jnp.zeros_like(accs)

    def build(i, skip):
        ec = coarse[i, 0]
        es = coarse[i, 1]
        for m in range(BLOCKS):
            c, s = rotate(ec, es, fine[0, m], fine[1, m])
            if skip > 128 * m:
                live = lane + 128 * m >= skip
                c = jnp.where(live, c, 0.0)
                s = jnp.where(live, s, 0.0)
            w_ref[i, :128, pl.ds(128 * m, 128)] = c.astype(BF16)
            w_ref[i, 128:, pl.ds(128 * m, 128)] = s.astype(BF16)

    def rows(block, first):
        return pl.ds(pl.multiple_of(HOP * block + first, 16), CHUNK)

    def block_zero(i, first):
        acc[...] += dot(w_ref[i], x_ref[rows(0, first), :], ((1,), (0,)))

    def early(i, carry):
        piece(0, i, CHUNK).wait()
        build(i, 0)
        block_zero(i, i * CHUNK)
        return carry

    final = CHUNKS - 1
    lax.fori_loop(0, final, early, 0)
    piece(0, final, HOP - CHUNK * final).wait()
    build(final, final * CHUNK - LAST)
    block_zero(final, LAST)

    def sum_row(values):
        folded = values[:, :128]
        for t in range(1, width // 128):
            folded = folded + values[:, 128 * t : 128 * t + 128]
        return jnp.sum(jnp.transpose(folded), axis=0, keepdims=True)

    def column(row):
        return jnp.transpose(jnp.broadcast_to(row, (128, 128)))

    def wide(tile):
        return jnp.concatenate([tile] * (width // 128), axis=1)

    for p in range(2):
        values = acc[pl.ds(128 * p, 128), :]
        row = sum_row(values)
        first_sum[pl.ds(p, 1), :] = row
        lump[pl.ds(128 * p, 128), :] = (values - wide(column(row) * (1.0 / width))).astype(BF16)
    first_sum[2:, :] = jnp.zeros((6, 128), F32)

    send_lump = pltpu.make_async_remote_copy(
        src_ref=lump,
        dst_ref=rest,
        send_sem=lump_send,
        recv_sem=lump_recv,
        device_id={"chan": me_c, "seg": before},
        device_id_type=MESH,
    )

    def send_first(i):
        return pltpu.make_async_remote_copy(
            src_ref=first_sum,
            dst_ref=first_sums.at[i],
            send_sem=first_send.at[i],
            recv_sem=first_recv.at[i],
            device_id={"chan": (me_c + i) % chans, "seg": before},
            device_id_type=MESH,
        )

    def send_sum(i):
        return pltpu.make_async_remote_copy(
            src_ref=own_sum,
            dst_ref=own_sums.at[i],
            send_sem=sum_send.at[i],
            recv_sem=sum_recv.at[i],
            device_id={"chan": (me_c + i) % chans, "seg": me_s},
            device_id_type=MESH,
        )

    def started(make):
        def body(i, carry):
            make(i).start()
            return carry
        return body

    def received(make):
        def body(i, carry):
            make(i).wait_recv()
            return carry
        return body

    def sent(make):
        def body(i, carry):
            make(i).wait_send()
            return carry
        return body

    lax.fori_loop(0, chans, started(send_first), 0)
    send_lump.start()

    def later(i, first):
        table = w_ref[i]
        for block in (1, 2):
            accs[block - 1] += dot(table, x_ref[rows(block, first), :256], ((1,), (0,)))
        tails = jnp.concatenate([x_ref[rows(1, first), 256:], x_ref[rows(2, first), 256:]], axis=1)
        accs[2] += dot(table, tails, ((1,), (0,)))

    def late(i, carry):
        for block in (1, 2):
            piece(block, i, CHUNK).wait()
        later(i, i * CHUNK)
        return carry

    lax.fori_loop(0, final, late, 0)
    for block in (1, 2):
        piece(block, final, HOP - CHUNK * final).wait()
    later(final, LAST)

    edge = w_ref[0, :, pl.ds(0, 128)].astype(F32)
    lane2 = lax.broadcasted_iota(jnp.int32, (256, 128), 1)
    alive = jnp.where(me_s == segs - 1, 0.0, 1.0).astype(F32)

    def swap(q, new, old):
        table = jnp.where(lane2 < offs_ref[q], edge, 0.0)
        both = jnp.concatenate([table, -table], axis=1).astype(BF16)
        head[...] = dot(both, jnp.concatenate([new, old], axis=0), ((1,), (0,)))

    def block_sum(p, parts):
        at = pl.ds(128 * p, 128)
        total = head[at, :]
        for factor, block in parts:
            if block == 0:
                values = acc[at, :]
            else:
                values = jnp.concatenate(
                    [accs[block - 1, at, :], accs[2, at, pl.ds(128 * (block - 1), 128)]], axis=1
                )
            total = total + (values if factor is None else values * factor)
        return total

    def finish(q, parts):
        c = block_sum(0, parts)
        s = block_sum(1, parts)
        c, s = rotate(c, s, wide(coarse[CHUNKS + q, 0]), wide(coarse[CHUNKS + q, 1]))
        spec[q, :128] = c
        spec[q, 128:] = s
        own_sum[pl.ds(2 * q, 1), :] = sum_row(c)
        own_sum[pl.ds(2 * q + 1, 1), :] = sum_row(s)

    def first_rows(block):
        return x_ref[pl.ds(HOP * block, 128), :]

    def rim_rows(k):
        return (rim[k].astype(F32) * alive).astype(BF16)

    own_sum[6:, :] = jnp.zeros((2, 128), F32)
    signs = wide(sign)
    swap(0, first_rows(2), first_rows(0))
    finish(0, [(None, 0), (signs, 1)])
    send_rim(0).wait_recv()
    swap(1, rim_rows(0), first_rows(1))
    finish(1, [(None, 1), (signs, 2)])
    send_rim(1).wait_recv()
    swap(2, rim_rows(1), first_rows(2))
    finish(2, [(None, 2)])
    lax.fori_loop(1, chans, started(send_sum), 0)

    lax.fori_loop(0, chans, received(send_first), 0)
    first_total = first_sums[0]
    for i in range(1, chans):
        first_total = first_total + first_sums[i]
    mine = first_sums[0] * (1.0 / width)
    send_lump.wait_recv()
    turn_c = coarse[CHUNKS + 2, 0]
    turn_s = coarse[CHUNKS + 2, 1]
    flip = sign * alive
    rest_c = (rest[:128, :].astype(F32) + wide(column(mine[0:1]))) * wide(flip)
    rest_s = (rest[128:, :].astype(F32) + wide(column(mine[1:2]))) * wide(flip)
    rest_c, rest_s = rotate(rest_c, rest_s, wide(turn_c), wide(turn_s))
    spec[2, :128] += rest_c
    spec[2, 128:] += rest_s

    lax.fori_loop(1, chans, received(send_sum), 0)
    total = own_sum[...]
    for i in range(1, chans):
        total = total + own_sums[i]
    scale = 1.0 / (width * chans)

    def send_part(q, i):
        g = (me_s + i) % segs
        return pltpu.make_async_remote_copy(
            src_ref=white.at[q, :, pl.ds(pl.multiple_of(16 * g, 16), 16), :],
            dst_ref=got.at[me_s, q, :, :, pl.ds(0, width)],
            send_sem=part_send.at[q, i],
            recv_sem=part_recv.at[q, i],
            device_id={"chan": me_c, "seg": g},
            device_id_type=MESH,
        )

    def take_part(q, i):
        g = (me_s + segs - i) % segs
        return pltpu.make_async_remote_copy(
            src_ref=white.at[q, :, pl.ds(0, 16), :],
            dst_ref=got.at[g, q, :, :, pl.ds(0, width)],
            send_sem=part_send.at[q, i],
            recv_sem=part_recv.at[q, i],
            device_id={"chan": me_c, "seg": g},
            device_id_type=MESH,
        )

    def send_near(q, i):
        g = (me_s + segs - i) % segs
        return pltpu.make_async_remote_copy(
            src_ref=got.at[g, q, :, :, pl.ds(0, 256)],
            dst_ref=got.at[g, q, :, :, pl.ds(width, 256)],
            send_sem=near_send.at[q, i],
            recv_sem=near_recv.at[q, i],
            device_id={"chan": left, "seg": me_s},
            device_id_type=MESH,
        )

    for q in range(3):
        mean_c = column(total[2 * q : 2 * q + 1] * scale)
        mean_s = column(total[2 * q + 1 : 2 * q + 2] * scale)
        if q == 2:
            more_c, more_s = rotate(
                column(first_total[0:1] * scale) * flip, column(first_total[1:2] * scale) * flip, turn_c, turn_s
            )
            mean_c = mean_c + more_c
            mean_s = mean_s + more_s
        c = spec[q, :128] - wide(mean_c)
        s = spec[q, 128:] - wide(mean_s)
        power = jnp.sum(c * c + s * s, axis=0, keepdims=True) * (1.0 / 256)
        gain = lax.rsqrt(power + 1e-06)
        white[q, 0] = (c * gain).astype(BF16)
        white[q, 1] = (s * gain).astype(BF16)
        lax.fori_loop(1, segs, started(lambda i: send_part(q, i)), 0)
        mine_at = pl.ds(pl.multiple_of(16 * me_s, 16), 16)
        for p in range(2):
            got[me_s, q, p, :, pl.ds(0, width)] = white[q, p, mine_at, :]
        send_near(q, 0).start()

    for q in range(3):
        def relay(i, carry):
            take_part(q, i).wait_recv()
            send_near(q, i).start()
            return carry
        lax.fori_loop(1, segs, relay, 0)
    for q in range(3):
        lax.fori_loop(0, segs, received(lambda i: send_near(q, i)), 0)
    shown = jnp.where(me_c == chans - 1, 0.0, 1.0).astype(F32)

    def put(g, carry):
        for q in range(3):
            for p in range(2):
                out_ref[g, q, p, :, pl.ds(0, width)] = got[g, q, p, :, pl.ds(0, width)]
                tail = got[g, q, p, :, pl.ds(width, 256)].astype(F32) * shown
                out_ref[g, q, p, :, pl.ds(width, 256)] = tail.astype(BF16)
        return carry

    lax.fori_loop(0, segs, put, 0)

    for k in range(2):
        send_rim(k).wait_send()
    send_lump.wait_send()
    lax.fori_loop(0, chans, sent(send_first), 0)
    lax.fori_loop(1, chans, sent(send_sum), 0)
    for q in range(3):
        lax.fori_loop(1, segs, sent(lambda i: send_part(q, i)), 0)
        lax.fori_loop(0, segs, sent(lambda i: send_near(q, i)), 0)


def spectra(offsets, bins, record, chans, segs):
    width = record.shape[1]
    vmem = pl.BlockSpec(memory_space=pltpu.VMEM)
    sems = pltpu.SemaphoreType.DMA
    return pl.pallas_call(
        functools.partial(spectra_kernel, chans, segs),
        out_shape=jax.ShapeDtypeStruct((segs, 3, 2, 16, width + 256), BF16),
        in_specs=[pl.BlockSpec(memory_space=pltpu.SMEM), vmem, pl.BlockSpec(memory_space=pl.ANY)],
        out_specs=vmem,
        scratch_shapes=[
            pltpu.VMEM(record.shape, BF16),
            pltpu.VMEM((2, BLOCKS, 128, 128), F32),
            pltpu.VMEM((CHUNKS + 3, 2, 128, 128), F32),
            pltpu.VMEM((CHUNKS, 256, CHUNK), BF16),
            pltpu.VMEM((256, width), F32),
            pltpu.VMEM((3, 256, 256), F32),
            pltpu.VMEM((3, 256, width), F32),
            pltpu.VMEM((256, width), F32),
            pltpu.VMEM((256, width), BF16),
            pltpu.VMEM((8, 128), F32),
            pltpu.VMEM((chans, 8, 128), F32),
            pltpu.VMEM((8, 128), F32),
            pltpu.VMEM((chans, 8, 128), F32),
            pltpu.VMEM((2, 128, width), BF16),
            pltpu.VMEM((256, width), BF16),
            pltpu.VMEM((3, 2, 128, width), BF16),
            pltpu.VMEM((segs, 3, 2, 16, width + 256), BF16),
            sems((3, CHUNKS)),
            sems((2,)),
            sems((2,)),
            sems(()),
            sems(()),
            sems((chans,)),
            sems((chans,)),
            sems((chans,)),
            sems((chans,)),
            sems((3, segs)),
            sems((3, segs)),
            sems((3, segs)),
            sems((3, segs)),
        ],
        compiler_params=pltpu.CompilerParams(
            vmem_limit_bytes=VMEM_LIMIT, collective_id=0, has_side_effects=True
        ),
        name="spectra",
    )(offsets, bins, record)


def band_kernel(scale, ext_ref, limit_ref, out_ref, own, rev, wide):
    tile = pl.program_id(0)
    segs = ext_ref.shape[0] // 32

    @pl.when(tile == 0)
    def _():
        size = rev.shape[0] * 128
        at = lax.broadcasted_iota(jnp.int32, (size, size), 0)
        to = lax.broadcasted_iota(jnp.int32, (size, size), 1)
        flip = (at + to == size - 1).astype(BF16)
        turned = dot(ext_ref[...], flip, ((1,), (0,)))
        for t in range(rev.shape[0]):
            for n in range(segs):
                rev[t, pl.ds(PITCH * n, 32)] = turned[32 * n : 32 * n + 32, 128 * t : 128 * t + 128]
        for t in range(own.shape[0]):
            for n in range(segs):
                own[t, pl.ds(PITCH * n, 32)] = ext_ref[32 * n : 32 * n + 32, 128 * t : 128 * t + 128].astype(F32)

    lag = lax.broadcasted_iota(jnp.int32, (208, 256), 0)
    spot = lax.broadcasted_iota(jnp.int32, (208, 256), 1)
    pick = (lag + spot == 255).astype(BF16)
    back = own.shape[0] - 1 - tile

    def one_bin(f, carry):
        real = own[tile, pl.ds(f, segs, stride=PITCH), :]
        imag = own[tile, pl.ds(16 + f, segs, stride=PITCH), :]
        lhs = jnp.concatenate(
            [jnp.concatenate([real, imag], axis=0), jnp.concatenate([imag, -real], axis=0)], axis=1
        ).astype(BF16)
        other = []
        for t in range(3):
            other.append(
                jnp.concatenate(
                    [rev[back + t, pl.ds(f, segs, stride=PITCH), :], rev[back + t, pl.ds(16 + f, segs, stride=PITCH), :]],
                    axis=0,
                )
            )
        rhs = jnp.concatenate(other, axis=1).astype(BF16)
        product = dot(lhs, rhs, ((0,), (0,)))
        lined = []
        for p in range(2):
            rolled = pltpu.roll(product[128 * p : 128 * p + 128], 0, 1, stride=1, stride_axis=0)
            lined.append((rolled[:, 128:] * scale).astype(BF16))
        by_lag = dot(pick, jnp.concatenate(lined, axis=0), ((1,), (1,)))
        wide[pl.ds(f, LAGS, stride=PITCH), :] = by_lag[:LAGS, :128]
        wide[pl.ds(16 + f, LAGS, stride=PITCH), :] = by_lag[:LAGS, 128:]
        return carry

    lax.fori_loop(0, 16, one_bin, 0, unroll=UNROLL)
    limit = jnp.broadcast_to(limit_ref[...], (32, 128))

    def store(j, carry):
        for n in range(8):
            k = j * 8 + n
            values = wide[pl.ds(k * PITCH, 32), :]
            values = jnp.where(limit >= k, values, 0.0).astype(BF16)
            out_ref[k, 0] = values[:16]
            out_ref[k, 1] = values[16:]
        return carry

    lax.fori_loop(0, LAGS // 8, store, 0)


def band(ext, limit, segs, width):
    rows, reach = ext.shape
    return pl.pallas_call(
        lambda *refs: band_kernel(1.0 / segs, *refs),
        grid=(width // 128,),
        out_shape=jax.ShapeDtypeStruct((LAGS, 2, 16, width), BF16),
        in_specs=[
            pl.BlockSpec((rows, reach), lambda i: (0, 0)),
            pl.BlockSpec((1, 128), lambda i: (0, i)),
        ],
        out_specs=pl.BlockSpec((LAGS, 2, 16, 128), lambda i: (0, 0, 0, i)),
        scratch_shapes=[
            pltpu.VMEM((width // 128, segs * PITCH, 128), F32),
            pltpu.VMEM((reach // 128, segs * PITCH, 128), F32),
            pltpu.VMEM((LAGS * PITCH, 128), F32),
        ],
        compiler_params=pltpu.CompilerParams(vmem_limit_bytes=VMEM_LIMIT),
        name="band",
    )(ext, limit)


def shards(record, offsets, bins, band_limit):
    width = record.shape[1]
    segs = lax.axis_size("seg")
    parts = spectra(offsets, bins[None, :], record, lax.axis_size("chan"), segs)
    ext = parts.reshape(segs * 96, width + 256)
    return band(ext, band_limit[None, :], segs * 3, width)


def solution(mesh):
    return jax.shard_map(
        shards,
        mesh=mesh,
        in_specs=(P("seg", "chan"), P("seg"), P(), P("chan")),
        out_specs=P(None, None, "seg", "chan"),
        check_vma=False,
    )
```

time: 142 us -> 62 us (0.44)
  blocking collectives: 48.2 us -> 0 us
  waiting for transfers between devices: 15.7 us -> 0 us
  starting transfers between devices: 12.8 us -> 0 us
  Pallas kernels: 52.9 us -> 60.6 us
  other arithmetic: 5.16 us -> 0 us
  local copies, waits for them, and re-layouts: 6.18 us -> 1.26 us
    psum x1 -> x0, blocking collectives: 29.9 us -> none  [shards(): mean = lax.psum(jnp.sum(spectra, axis=2), 'chan') / channels]
    pallas_call x1, Pallas kernels: 16.8 us -> 40.8 us  [spectra(): pl.pallas_call(functools.partial(spectra_kernel, chans, segs), out_shape=...]
    all_to_all x1 -> x0, blocking collectives: 18.4 us -> none  [shards(): lax.all_to_all(white, 'seg', split_axis=2, concat_axis=0, tiled=True)]
    pallas_call x1, Pallas kernels: 36.1 us -> 19.8 us  [band(): pl.pallas_call(lambda *refs: band_kernel(1.0 / segs, *refs), grid=(width...]
    ppermute x4 -> x0, waiting for transfers between devices: 15.7 us -> none  [along(): return lax.ppermute(shard, axis, pairs)]
    ppermute x4 -> x0, starting transfers between devices: 12.8 us -> none  [along(): return lax.ppermute(shard, axis, pairs)]
    concatenate x2 -> x0, other arithmetic: 2.93 us -> none  [the longest x1 1.88 us: shards(): offs = jnp.concatenate([before[2:], offsets])]
    slice x4 -> x0, local copies, waits for them, and re-layouts: 2.71 us -> none  [the longest x1 1.19 us: shards(): spectra = jnp.stack([parts[1], parts[2], parts[3] + rest])]
  transfers between devices with their start and end apart: 4 -> 0, of which waited for: 3 -> 0; matrix products, arithmetic and copies ran while one was open for 4% -> 0% of each run, Pallas kernels for 0% -> 0%
where the time goes in v2:
time: 62 us; the launch traced here: 61.9 us
  Pallas kernels  60.6 us (98%)
  local copies, waits for them, and re-layouts  1.26 us (2%)
    pallas_call x1, Pallas kernels, spectra(): pl.pallas_call(functools.partial(spectra_kernel, chans, segs), out_shape=...  40.8 us
    pallas_call x1, Pallas kernels, band(): pl.pallas_call(lambda *refs: band_kernel(1.0 / segs, *refs), grid=(width...  19.8 us
    broadcast_in_dim x1, local copies, waits for them, and re-layouts, shards(): return band(ext, band_limit[None, :], segs * 3, width)  1.26 us

profile of v2, /device:TPU:1, one launch (start us, length us, event | category | flops | bytes accessed | tf_op | source)
XLA Modules:
  0.0 61.9 jit_solution(6483253644747939005)
XLA Ops:
  0.0 1.3 %broadcast_in_dim.7.refs_1_ = s32[1,384]{1,0:T(1,128)} reshape(s32[384]{0:T(512)} %param.7) | data formatting | bytes 3072 | tf_op jit(solution)/shard_map/broadcast_in_dim | solution.py:530
  1.3 40.8 %spectra.1 = bf16[8,3,2,16,640]{4,3,2,1,0:T(8,128)(2,1)} custom-call(s32[3]{0:T(128)} %offs_ref.1, s32[1,128]{1,0:T(1,128)} %bitcast.3, bf16[18000,384]{1,0:T(8,128)(2,1)} %rec_ref.1), custom_call_target="tpu_custom_call" | custom-call | tf_op jit(solution)/shard_map/spectra/pallas_call | solution.py:397
  42.0 19.8 %band.1 = bf16[200,2,16,384]{3,2,1,0:T(8,128)(2,1)} custom-call(bf16[768,640]{1,0:T(8,128)(2,1)} %bitcast.2, s32[1,384]{1,0:T(1,128)} %broadcast_in_dim.7.refs_1_), custom_call_target="tpu_custom_call" | custom-call | tf_op jit(solution)/shard_map/band/pallas_call | solution.py:506

commit v3 on v2

--- a/solution.py
+++ b/solution.py
@@ -31,14 +31,13 @@
 def spectra_kernel(
     chans, segs, offs_ref, bins_ref, rec_ref, out_ref,
     x_ref, fine, coarse, w_ref, acc, accs, spec, head, lump, first_sum, first_sums, own_sum, own_sums,
-    rim, rest, white, got,
-    local_sem, rim_send, rim_recv, lump_send, lump_recv, first_send, first_recv, sum_send, sum_recv,
+    rest_sum, group_sum, rim, rest, white, got,
+    local_sem, rim_send, rim_recv, row_send, row_recv, lump_send, lump_recv, first_send, first_recv, sum_send, sum_recv,
     part_send, part_recv, near_send, near_recv,
 ):
     me_c = lax.axis_index("chan")
     me_s = lax.axis_index("seg")
     before = (me_s + segs - 1) % segs
-    after = (me_s + 1) % segs
     left = (me_c + chans - 1) % chans
     width = x_ref.shape[1]
 
@@ -50,10 +49,7 @@
         pl.semaphore_signal(barrier, inc=1, device_id={"chan": c, "seg": g}, device_id_type=MESH)
 
     def greet_chan(i, carry):
-        c = (me_c + i) % chans
-        greet(c, me_s)
-        greet(c, before)
-        greet(c, after)
+        greet((me_c + i) % chans, me_s)
         return carry
 
     def greet_seg(i, carry):
@@ -101,8 +97,6 @@
     odd = bcol % 2
     sign = (1 - 2 * odd).astype(F32)
 
-    pl.semaphore_wait(barrier, 3 * (chans - 1) + segs - 1)
-
     def send_rim(k):
         return pltpu.make_async_remote_copy(
             src_ref=rec_ref.at[pl.ds(HOP * k, RIM)],
@@ -112,9 +106,6 @@
             device_id={"chan": me_c, "seg": before},
             device_id_type=MESH,
         )
-
-    for k in range(2):
-        send_rim(k).start()
 
     acc[...] = jnp.zeros_like(acc)
     accs[...] = jnp.zeros_like(accs)
@@ -183,7 +174,7 @@
             dst_ref=first_sums.at[i],
             send_sem=first_send.at[i],
             recv_sem=first_recv.at[i],
-            device_id={"chan": (me_c + i) % chans, "seg": before},
+            device_id={"chan": (me_c + i) % chans, "seg": me_s},
             device_id_type=MESH,
         )
 
@@ -215,8 +206,22 @@
             return carry
         return body
 
-    lax.fori_loop(0, chans, started(send_first), 0)
+    def send_row(k, source):
+        return pltpu.make_async_remote_copy(
+            src_ref=source,
+            dst_ref=rest_sum.at[k],
+            send_sem=row_send.at[k],
+            recv_sem=row_recv.at[k],
+            device_id={"chan": me_c, "seg": before},
+            device_id_type=MESH,
+        )
+
+    pl.semaphore_wait(barrier, chans + segs - 2)
+    lax.fori_loop(1, chans, started(send_first), 0)
+    send_row(0, first_sum).start()
     send_lump.start()
+    for k in range(2):
+        send_rim(k).start()
 
     def later(i, first):
         table = w_ref[i]
@@ -235,6 +240,13 @@
     for block in (1, 2):
         piece(block, final, HOP - CHUNK * final).wait()
     later(final, LAST)
+
+    lax.fori_loop(1, chans, received(send_first), 0)
+    first_total = first_sum[...]
+    for i in range(1, chans):
+        first_total = first_total + first_sums[i]
+    group_sum[...] = first_total
+    send_row(1, group_sum).start()
 
     edge = w_ref[0, :, pl.ds(0, 128)].astype(F32)
     lane2 = lax.broadcasted_iota(jnp.int32, (256, 128), 1)
@@ -285,11 +297,9 @@
     finish(2, [(None, 2)])
     lax.fori_loop(1, chans, started(send_sum), 0)
 
-    lax.fori_loop(0, chans, received(send_first), 0)
-    first_total = first_sums[0]
-    for i in range(1, chans):
-        first_total = first_total + first_sums[i]
-    mine = first_sums[0] * (1.0 / width)
+    scale = 1.0 / (width * chans)
+    send_row(0, first_sum).wait_recv()
+    mine = rest_sum[0] * (1.0 / width)
     send_lump.wait_recv()
     turn_c = coarse[CHUNKS + 2, 0]
     turn_s = coarse[CHUNKS + 2, 1]
@@ -301,10 +311,11 @@
     spec[2, 128:] += rest_s
 
     lax.fori_loop(1, chans, received(send_sum), 0)
+    send_row(1, group_sum).wait_recv()
+    behind = rest_sum[1] * scale
     total = own_sum[...]
     for i in range(1, chans):
         total = total + own_sums[i]
-    scale = 1.0 / (width * chans)
 
     def send_part(q, i):
         g = (me_s + i) % segs
@@ -344,7 +355,7 @@
         mean_s = column(total[2 * q + 1 : 2 * q + 2] * scale)
         if q == 2:
             more_c, more_s = rotate(
-                column(first_total[0:1] * scale) * flip, column(first_total[1:2] * scale) * flip, turn_c, turn_s
+                column(behind[0:1]) * flip, column(behind[1:2]) * flip, turn_c, turn_s
             )
             mean_c = mean_c + more_c
             mean_s = mean_s + more_s
@@ -383,7 +394,9 @@
     for k in range(2):
         send_rim(k).wait_send()
     send_lump.wait_send()
-    lax.fori_loop(0, chans, sent(send_first), 0)
+    lax.fori_loop(1, chans, sent(send_first), 0)
+    send_row(0, first_sum).wait_send()
+    send_row(1, group_sum).wait_send()
     lax.fori_loop(1, chans, sent(send_sum), 0)
     for q in range(3):
         lax.fori_loop(1, segs, sent(lambda i: send_part(q, i)), 0)
@@ -413,11 +426,15 @@
             pltpu.VMEM((chans, 8, 128), F32),
             pltpu.VMEM((8, 128), F32),
             pltpu.VMEM((chans, 8, 128), F32),
+            pltpu.VMEM((2, 8, 128), F32),
+            pltpu.VMEM((8, 128), F32),
             pltpu.VMEM((2, 128, width), BF16),
             pltpu.VMEM((256, width), BF16),
             pltpu.VMEM((3, 2, 128, width), BF16),
             pltpu.VMEM((segs, 3, 2, 16, width + 256), BF16),
             sems((3, CHUNKS)),
+            sems((2,)),
+            sems((2,)),
             sems((2,)),
             sems((2,)),
             sems(()),
@@ -487,7 +504,7 @@
         return carry
 
     lax.fori_loop(0, 16, one_bin, 0, unroll=UNROLL)
-    limit = jnp.broadcast_to(limit_ref[...], (32, 128))
+    limit = jnp.broadcast_to(limit_ref[pl.ds(pl.multiple_of(tile * 128, 128), 128)].reshape(1, 128), (32, 128))
 
     def store(j, carry):
         for n in range(8):
@@ -509,7 +526,7 @@
         out_shape=jax.ShapeDtypeStruct((LAGS, 2, 16, width), BF16),
         in_specs=[
             pl.BlockSpec((rows, reach), lambda i: (0, 0)),
-            pl.BlockSpec((1, 128), lambda i: (0, i)),
+            pl.BlockSpec((width,), lambda i: (0,)),
         ],
         out_specs=pl.BlockSpec((LAGS, 2, 16, 128), lambda i: (0, 0, 0, i)),
         scratch_shapes=[
@@ -527,7 +544,7 @@
     segs = lax.axis_size("seg")
     parts = spectra(offsets, bins[None, :], record, lax.axis_size("chan"), segs)
     ext = parts.reshape(segs * 96, width + 256)
-    return band(ext, band_limit[None, :], segs * 3, width)
+    return band(ext, band_limit, segs * 3, width)
 
 
 def solution(mesh):

time: 62 us -> 61.3 us (0.989)
  local copies, waits for them, and re-layouts: 1.26 us -> 0 us
    broadcast_in_dim x1 -> x0, local copies, waits for them, and re-layouts: 1.26 us -> none  [shards(): return band(ext, band_limit[None, :], segs * 3, width)]
where the time goes in v3:
time: 61.3 us; the launch traced here: 61.1 us
  Pallas kernels  61.1 us (100%)
    pallas_call x1, Pallas kernels, spectra(): pl.pallas_call(functools.partial(spectra_kernel, chans, segs), out_shape=...  41.3 us
    pallas_call x1, Pallas kernels, band(): pl.pallas_call(lambda *refs: band_kernel(1.0 / segs, *refs), grid=(width...  19.8 us

profile of v3, /device:TPU:1, one launch (start us, length us, event | category | flops | bytes accessed | tf_op | source)
XLA Modules:
  0.0 61.1 jit_solution(7375018737051972228)
XLA Ops:
  0.0 41.3 %spectra.1 = bf16[8,3,2,16,640]{4,3,2,1,0:T(8,128)(2,1)} custom-call(s32[3]{0:T(128)} %offs_ref.1, s32[1,128]{1,0:T(1,128)} %bitcast.3, bf16[18000,384]{1,0:T(8,128)(2,1)} %rec_ref.1), custom_call_target="tpu_custom_call" | custom-call | tf_op jit(solution)/shard_map/spectra/pallas_call | solution.py:410
  41.3 19.8 %band.1 = bf16[200,2,16,384]{3,2,1,0:T(8,128)(2,1)} custom-call(bf16[768,640]{1,0:T(8,128)(2,1)} %bitcast.2, s32[384]{0:T(512)} %refs_1_.1), custom_call_target="tpu_custom_call" | custom-call | tf_op jit(solution)/shard_map/band/pallas_call | solution.py:523
